TPU v7x, 128 devices: a whole 4x4x4 slice. The times are simulated.
128 devices in a mesh: row: 8 (over z, y_hi), col: 16 (over x, y_lo, core).
Axes of the slice: x: 4, y: 4 (y_hi: 2, y_lo: 2; y = y_hi * 2 + y_lo), z: 4, core: 2. Of those that a mesh axis runs over, the one named last changes fastest.
Arguments:
- tokens: bfloat16 [1536, 14336], P('col', 'row'), may hold values from -6 to 6
- weight_in: bfloat16 [14336, 14336], P('row', 'col'), may hold values from -0.046875 to 0.046875
- bias_hidden: float32 [14336], P('col'), may hold values from -3 to 3
- weight_out: bfloat16 [14336, 14336], P('col', 'row'), may hold values from -0.046875 to 0.046875
- out_grad: bfloat16 [1536, 14336], P('col', 'row'), may hold values from -0.75 to 0.75
Outputs:
- grad_tokens: bfloat16 [1536, 14336], P('col', 'row')
- grad_weight_in: float32 [14336, 14336], P('row', 'col')
- grad_bias: float32 [14336], P('col')
- grad_weight_out: float32 [14336, 14336], P('col', 'row')
All inputs are finite; a program needn't handle non-finite values.
Results may differ from a plain program's by a relative error of at most 0.007.
Values may be sent and summed in bfloat16 or wider, within the bound.
A program may use at most 128 MiB of HBM per device.

v0:
```python
import jax
import jax.numpy as jnp
from jax import lax
from jax.sharding import PartitionSpec as P

GELU_SCALE = 0.7978845608
GELU_CUBIC = 0.044715


def gelu_parts(values):
    inner = GELU_SCALE * (values + GELU_CUBIC * values * values * values)
    tangent = jnp.tanh(inner)
    result = 0.5 * values * (1.0 + tangent)
    slope = 0.5 * (1.0 + tangent) + 0.5 * values * (1.0 - tangent * tangent) * GELU_SCALE * (
        1.0 + 3.0 * GELU_CUBIC * values * values
    )
    return (result, slope)


def contract_rows(left, right):
    return lax.dot_general(
        left, right, (((0,), (0,)), ((), ())), preferred_element_type=jnp.float32
    )


def contract_cols(left, right):
    return lax.dot_general(
        left, right, (((1,), (1,)), ((), ())), preferred_element_type=jnp.float32
    )


def local(tokens, weight_in, bias_hidden, weight_out, out_grad):
    tok_all, grad_all = (
        lax.all_gather(tokens, "col", axis=0, tiled=True),
        lax.all_gather(out_grad, "col", axis=0, tiled=True),
    )
    pre_part = jnp.dot(tok_all, weight_in, preferred_element_type=jnp.float32)
    act_part = contract_cols(grad_all, weight_out)
    pre_mine, act_mine = (
        lax.psum_scatter(pre_part, "row", scatter_dimension=0, tiled=True),
        lax.psum_scatter(act_part, "row", scatter_dimension=0, tiled=True),
    )
    result, slope = gelu_parts(pre_mine + bias_hidden)
    act_local = result.astype(jnp.bfloat16)
    pre_grad_local = (act_mine * slope).astype(jnp.bfloat16)
    bias_local = jnp.sum(pre_grad_local, axis=0, dtype=jnp.float32)
    act_all, pre_grad_all = (
        lax.all_gather(act_local, "row", axis=0, tiled=True),
        lax.all_gather(pre_grad_local, "row", axis=0, tiled=True),
    )
    grad_bias = lax.psum(bias_local, "row")
    grad_weight_out = contract_rows(act_all, grad_all)
    grad_weight_in = contract_rows(tok_all, pre_grad_all)
    grad_tokens = lax.psum_scatter(
        contract_cols(pre_grad_all, weight_in), "col", scatter_dimension=0, tiled=True
    ).astype(jnp.bfloat16)
    return (grad_tokens, grad_weight_in, grad_bias, grad_weight_out)


def solution(mesh):
    placed = (P("col", "row"), P("row", "col"), P("col"), P("col", "row"), P("col", "row"))
    return jax.shard_map(
        local,
        mesh=mesh,
        in_specs=placed,
        out_specs=(P("col", "row"), P("row", "col"), P("col"), P("col", "row")),
        check_vma=False,
    )
```

profile of v0, /device:TPU:1, one launch (start us, length us, event | category | flops | bytes accessed | tf_op | source)
XLA Modules:
  0.0 540.9 jit_solution(17161725866408645790)
XLA Ops:
  7.2 0.0 copy-start
  7.2 0.0 all-gather.5.cloned.1.call-start
  7.2 0.7 all-gather.5.cloned.1.call-update
  7.9 0.0 all-gather.7.cloned.1.call-start
  8.0 0.7 all-gather.7.cloned.1.call-update
  8.7 0.0 reduce-scatter.4.cloned.1.call-start
  8.7 44.7 %all-gather.5.cloned.1.call-done = bf16[1536,1792]{1,0:T(8,128)(2,1)} async-done(((bf16[96,1792]{1,0:T(8,128)(2,1)}), bf16[1536,1792]{1,0:T(8,128)(2,1)}) %all-gather.5.cloned.1.call-update) | async-done | bytes 5505040 | tf_op jit(solution)/shard_map/all_gather | solution.py:35
  53.4 10.3 %fusion.8 = f32[1536,896]{1,0:T(8,128)} fusion(bf16[1536,1792]{1,0:T(8,128)(2,1)} %all-gather.5.cloned.1.call-done, bf16[896,1792]{1,0:T(8,128)(2,1)} %param.8), kind=kOutput, calls=%fused_computation.12 | convolution fusion | flops 4932501504 | bytes 14221312 | tf_op jit(solution)/shard_map/dot_general | solution.py:27
  63.8 0.0 reduce-scatter.4.cloned.1.call-update
  63.8 0.0 reduce-scatter.6.cloned.1.call-start
  63.8 31.1 %all-gather.7.cloned.1.call-done = bf16[1536,1792]{1,0:T(8,128)(2,1)} async-done(((bf16[96,1792]{1,0:T(8,128)(2,1)}), bf16[1536,1792]{1,0:T(8,128)(2,1)}) %all-gather.7.cloned.1.call-update) | async-done | bytes 5505040 | tf_op jit(solution)/shard_map/all_gather | solution.py:34
  94.9 0.0 copy-done
  94.9 9.3 %fusion.9 = f32[1536,896]{1,0:T(8,128)} fusion(bf16[1536,1792]{1,0:T(8,128)(2,1)} %all-gather.7.cloned.1.call-done, bf16[1792,896]{1,0:T(8,128)(2,1)S(1)} %copy-done), kind=kOutput, calls=%fused_computation.13 | convolution fusion | flops 4932501504 | bytes 14221312 | tf_op jit(solution)/shard_map/dot_general | solution.py:37
  104.2 0.0 copy-start.2
  104.3 0.0 reduce-scatter.6.cloned.1.call-update
  104.3 0.0 all-gather.9.cloned.1.call-start
  104.3 86.9 %reduce-scatter.4.cloned.1.call-done = f32[192,896]{1,0:T(8,128)} async-done(((f32[1536,896]{1,0:T(8,128)}), f32[192,896]{1,0:T(8,128)}) %reduce-scatter.4.cloned.1.call-update) | async-done | bytes 688144 | tf_op jit(solution)/shard_map/reduce_scatter | solution.py:41
  191.2 96.3 %reduce-scatter.6.cloned.1.call-done = f32[192,896]{1,0:T(8,128)} async-done(((f32[1536,896]{1,0:T(8,128)}), f32[192,896]{1,0:T(8,128)}) %reduce-scatter.6.cloned.1.call-update) | async-done | bytes 688144 | tf_op jit(solution)/shard_map/reduce_scatter | solution.py:40
  287.5 0.0 copy-done.2
  287.5 2.7 convert_reduce_fusion
  290.2 0.0 all-gather.9.cloned.1.call-update
  290.2 0.0 all-gather.11.cloned.1.call-start
  290.3 0.5 all-gather.11.cloned.1.call-update
  290.8 0.0 reduce-scatter.8.cloned.1.call-start
  290.8 57.9 %all-gather.9.cloned.1.call-done = bf16[1536,896]{1,0:T(8,128)(2,1)} async-done(((bf16[192,896]{1,0:T(8,128)(2,1)}), bf16[1536,896]{1,0:T(8,128)(2,1)}) %all-gather.9.cloned.1.call-update) | async-done | bytes 2752528 | tf_op jit(solution)/shard_map/all_gather | solution.py:49
  348.8 9.9 %fusion.10 = f32[1536,1792]{1,0:T(8,128)} fusion(bf16[1536,896]{1,0:T(8,128)(2,1)} %all-gather.9.cloned.1.call-done, bf16[1792,896]{1,0:T(8,128)(2,1)S(1)} %copy-done), kind=kOutput, calls=%fused_computation.14 | convolution fusion | flops 4932501504 | bytes 16973824 | tf_op jit(solution)/shard_map/dot_general | solution.py:27
  358.7 0.0 copy-start.3
  358.7 0.0 reduce-scatter.8.cloned.1.call-update
  358.7 17.6 %psum.7 = f32[896]{0:T(1024)} all-reduce(f32[896]{0:T(1024)S(1)} %get-tuple-element.8), channel_id=1, replica_groups=mesh['row'=8,'col'=16] {'row'}, use_global_device_ids=true, to_apply=%region_4.0 | all-reduce | flops 896 | bytes 7168 | tf_op jit(solution)/shard_map/psum | solution.py:51
  376.3 0.0 copy-done.3
  376.3 10.5 %convolution_bitcast_fusion = f32[1792,896]{0,1:T(8,128)} fusion(bf16[1536,896]{1,0:T(8,128)(2,1)S(1)} %copy-done.3, bf16[1536,1792]{1,0:T(8,128)(2,1)} %all-gather.7.cloned.1.call-done), kind=kOutput, calls=%fused_computation | convolution fusion | flops 4932501504 | bytes 14680064 | tf_op jit(solution)/shard_map/dot_general | solution.py:21
  386.8 0.0 copy-start.1
  386.8 8.0 %copy.9 = f32[1792,896]{1,0:T(8,128)} copy(f32[1792,896]{0,1:T(8,128)} %convolution_bitcast_fusion) | data formatting | bytes 12845056
  394.8 13.5 %all-gather.11.cloned.1.call-done = bf16[1536,896]{1,0:T(8,128)(2,1)} async-done(((bf16[192,896]{1,0:T(8,128)(2,1)}), bf16[1536,896]{1,0:T(8,128)(2,1)}) %all-gather.11.cloned.1.call-update) | async-done | bytes 2752528 | tf_op jit(solution)/shard_map/all_gather | solution.py:48
  408.3 11.4 %fusion.11 = f32[896,1792]{1,0:T(8,128)} fusion(bf16[1536,896]{1,0:T(8,128)(2,1)} %all-gather.11.cloned.1.call-done, bf16[1536,1792]{1,0:T(8,128)(2,1)} %all-gather.5.cloned.1.call-done), kind=kOutput, calls=%fused_computation.15 | convolution fusion | flops 4932501504 | bytes 14680064 | tf_op jit(solution)/shard_map/dot_general | solution.py:21
  419.7 112.5 %reduce-scatter.8.cloned.1.call-done = f32[96,1792]{1,0:T(8,128)} async-done(((f32[1536,1792]{1,0:T(8,128)}), f32[96,1792]{1,0:T(8,128)}) %reduce-scatter.8.cloned.1.call-update) | async-done | bytes 688144 | tf_op jit(solution)/shard_map/reduce_scatter | solution.py:54
  532.2 1.9 convert_element_type.13
  534.0 0.0 copy-done.1
Async XLA Ops:
  7.2 87.8 %copy-start = (bf16[1792,896]{1,0:T(8,128)(2,1)S(1)}, bf16[1792,896]{1,0:T(8,128)(2,1)}, u32[]{:S(2)}) copy-start(bf16[1792,896]{1,0:T(8,128)(2,1)} %param.6) | copy-start | bytes 9633796
  7.2 46.2 %all-gather.5.cloned.1.call-start = ((), (), s32[]{:S(2)}) async-start(), calls=%async_computation.3 | async-start | bytes 5849088 | tf_op jit(solution)/shard_map/all_gather | solution.py:35
  7.9 87.0 %all-gather.7.cloned.1.call-start = ((), (), s32[]{:S(2)}) async-start(), calls=%async_computation.5 | async-start | bytes 5849088 | tf_op jit(solution)/shard_map/all_gather | solution.py:34
  8.7 182.5 %reduce-scatter.4.cloned.1.call-start = ((), (), s32[]{:S(2)}) async-start(), calls=%async_computation.4 | async-start | bytes 6193152 | tf_op jit(solution)/shard_map/reduce_scatter | solution.py:41
  63.8 223.7 %reduce-scatter.6.cloned.1.call-start = ((), (), s32[]{:S(2)}) async-start(), calls=%async_computation.6 | async-start | bytes 6193152 | tf_op jit(solution)/shard_map/reduce_scatter | solution.py:40
  104.2 183.3 %copy-start.2 = (f32[896]{0:T(1024)S(1)}, f32[896]{0:T(1024)}, u32[]{:S(2)}) copy-start(f32[896]{0:T(1024)} %param.7) | copy-start | bytes 10756
  104.3 244.5 %all-gather.9.cloned.1.call-start = ((), (), s32[]{:S(2)}) async-start(), calls=%async_computation.7 | async-start | bytes 3096576 | tf_op jit(solution)/shard_map/all_gather | solution.py:49
  290.2 118.1 %all-gather.11.cloned.1.call-start = ((), (), s32[]{:S(2)}) async-start(), calls=%async_computation.9 | async-start | bytes 3096576 | tf_op jit(solution)/shard_map/all_gather | solution.py:48
  290.8 241.4 %reduce-scatter.8.cloned.1.call-start = ((), (), s32[]{:S(2)}) async-start(), calls=%async_computation.8 | async-start | bytes 11698176 | tf_op jit(solution)/shard_map/reduce_scatter | solution.py:54
  358.7 17.6 %copy-start.3 = (bf16[1536,896]{1,0:T(8,128)(2,1)S(1)}, bf16[1536,896]{1,0:T(8,128)(2,1)}, u32[]{:S(2)}) copy-start(bf16[1536,896]{1,0:T(8,128)(2,1)} %all-gather.9.cloned.1.call-done) | copy-start | bytes 8257540
  386.8 147.2 %copy-start.1 = (bf16[1792,896]{1,0:T(8,128)(2,1)S(1)}, bf16[1792,896]{1,0:T(8,128)(2,1)}, u32[]{:S(2)}) copy-start(bf16[1792,896]{1,0:T(8,128)(2,1)} %param.6) | copy-start | bytes 9633796
Sparse Core Ops, SparseCore 0:
  9.7 43.6 all-gather.4
  55.1 39.7 all-gather.6
  99.4 91.7 reduce-scatter.3
  196.0 91.4 reduce-scatter.5
  290.3 58.3 all-gather.8
  350.9 57.3 all-gather.10
  410.7 121.3 reduce-scatter.7
where the time goes:
time: 541 us
  waiting for transfers between devices  445 us (82%)
  matrix products  51.5 us (10%)
  blocking collectives  17.6 us (3%)
  between operations  14.1 us (3%)
  local copies, waits for them, and re-layouts  7.99 us (1%)
    reduce_scatter x1, waiting for transfers between devices, local(): lax.psum_scatter(contract_cols(pre_grad_all, weight_in), 'col', scatter_d...  112 us
    reduce_scatter x1, waiting for transfers between devices, local(): lax.psum_scatter(pre_part, 'row', scatter_dimension=0, tiled=True)  96.3 us
    reduce_scatter x1, waiting for transfers between devices, local(): lax.psum_scatter(act_part, 'row', scatter_dimension=0, tiled=True)  86.9 us
    all_gather x1, waiting for transfers between devices, local(): lax.all_gather(pre_grad_local, 'row', axis=0, tiled=True)  57.9 us
    all_gather x1, waiting for transfers between devices, local(): lax.all_gather(out_grad, 'col', axis=0, tiled=True)  44.7 us
    all_gather x1, waiting for transfers between devices, local(): lax.all_gather(tokens, 'col', axis=0, tiled=True)  31.1 us
    dot_general x2, matrix products, contract_rows(): lax.dot_general(left, right, (((0,), (0,)), ((), ())), preferred_element_...  21.9 us
    dot_general x2, matrix products, contract_cols(): lax.dot_general(left, right, (((1,), (1,)), ((), ())), preferred_element_...  20.2 us
  transfers between devices with their start and end apart: 7, of which 7 were waited for; matrix products, arithmetic and copies ran while one was open for 11% of the time, Pallas kernels for 0%

commit v1 on v0

--- a/solution.py
+++ b/solution.py
@@ -30,8 +30,12 @@
 
 
 def local(tokens, weight_in, bias_hidden, weight_out, out_grad):
+    see_sources_all = lambda array_here, peer_axis, dim_i: jnp.concatenate(
+        lax.all_to_all(jnp.stack(lax.axis_size(peer_axis) * [array_here]), peer_axis, 0, 0),
+        axis=dim_i,
+    )
     tok_all, grad_all = (
-        lax.all_gather(tokens, "col", axis=0, tiled=True),
+        see_sources_all(tokens, "col", 0),
         lax.all_gather(out_grad, "col", axis=0, tiled=True),
     )
     pre_part = jnp.dot(tok_all, weight_in, preferred_element_type=jnp.float32)

time: 541 us -> 520 us (0.961)
  waiting for transfers between devices: 445 us -> 317 us
  blocking collectives: 17.6 us -> 119 us
    all_to_all x0 -> x1, blocking collectives: none -> 95.1 us  [local(): lax.all_to_all(jnp.stack(lax.axis_size(peer_axis) * [array_here]), peer_a...]
    all_gather x1, waiting for transfers between devices: 44.7 us -> 0.02 us  [local(): lax.all_gather(out_grad, 'col', axis=0, tiled=True)]
    reduce_scatter x1, waiting for transfers between devices: 112 us -> 68.5 us  [local(): lax.psum_scatter(contract_cols(pre_grad_all, weight_in), 'col', scatter_d...]
    all_gather x1 -> x0, waiting for transfers between devices: 31.1 us -> none  [local(): lax.all_gather(tokens, 'col', axis=0, tiled=True)]
    reduce_scatter x1, waiting for transfers between devices: 96.3 us -> 81.3 us  [local(): lax.psum_scatter(pre_part, 'row', scatter_dimension=0, tiled=True)]
    reduce_scatter x1, waiting for transfers between devices: 86.9 us -> 95.8 us  [local(): lax.psum_scatter(act_part, 'row', scatter_dimension=0, tiled=True)]
    psum x1, blocking collectives: 17.6 us -> 23.8 us  [local(): grad_bias = lax.psum(bias_local, 'row')]
  transfers between devices with their start and end apart: 7 -> 6, of which waited for: 7 -> 5; matrix products, arithmetic and copies ran while one was open for 11% -> 12% of each run, Pallas kernels for 0% -> 0%
where the time goes in v1:
time: 520 us
  waiting for transfers between devices  317 us (61%)
  blocking collectives  119 us (23%)
  matrix products  50.9 us (10%)
  between operations  15.7 us (3%)
  local copies, waits for them, and re-layouts  11.9 us (2%)
    reduce_scatter x1, waiting for transfers between devices, local(): lax.psum_scatter(act_part, 'row', scatter_dimension=0, tiled=True)  95.8 us
    all_to_all x1, blocking collectives, local(): lax.all_to_all(jnp.stack(lax.axis_size(peer_axis) * [array_here]), peer_a...  95.1 us
    reduce_scatter x1, waiting for transfers between devices, local(): lax.psum_scatter(pre_part, 'row', scatter_dimension=0, tiled=True)  81.3 us
    reduce_scatter x1, waiting for transfers between devices, local(): lax.psum_scatter(contract_cols(pre_grad_all, weight_in), 'col', scatter_d...  68.5 us
    all_gather x1, waiting for transfers between devices, local(): lax.all_gather(pre_grad_local, 'row', axis=0, tiled=True)  57.4 us
    psum x1, blocking collectives, local(): grad_bias = lax.psum(bias_local, 'row')  23.8 us
    dot_general x2, matrix products, contract_rows(): lax.dot_general(left, right, (((0,), (0,)), ((), ())), preferred_element_...  23.1 us
    dot_general x2, matrix products, contract_cols(): lax.dot_general(left, right, (((1,), (1,)), ((), ())), preferred_element_...  20.3 us
  transfers between devices with their start and end apart: 6, of which 5 were waited for; matrix products, arithmetic and copies ran while one was open for 12% of the time, Pallas kernels for 0%

profile of v1, /device:TPU:1, one launch (start us, length us, event | category | flops | bytes accessed | tf_op | source)
XLA Modules:
  0.0 519.6 jit_solution(8241186705899221400)
XLA Ops:
  8.0 0.0 copy-start
  8.0 0.0 all-gather.4.cloned.1.call-start
  8.1 0.7 all-gather.4.cloned.1.call-update
  8.7 0.0 reduce-scatter.6.cloned.1.call-start
  8.8 1.7 stack.2
  10.5 95.1 %all_to_all.5 = bf16[16,96,1792]{2,1,0:T(8,128)(2,1)S(1)} all-to-all(bf16[16,96,1792]{2,1,0:T(8,128)(2,1)S(1)} %stack.2), channel_id=1, replica_groups=mesh['row'=8,'col'=16] {'col'}, dimensions={0} | all-to-all | bytes 11010048 | tf_op jit(solution)/shard_map/all_to_all | solution.py:34
  105.5 0.0 copy-start.1
  105.5 2.4 copy-done.1
  107.9 0.0 copy-done
  107.9 7.6 %fusion.9 = f32[1536,896]{1,0:T(8,128)} fusion(bf16[1536,1792]{1,0:T(8,128)(2,1)S(1)} %bitcast.13, bf16[1792,896]{1,0:T(8,128)(2,1)S(1)} %copy-done), kind=kOutput, calls=%fused_computation.13 | convolution fusion | flops 4932501504 | bytes 14221312 | tf_op jit(solution)/shard_map/dot_general | solution.py:41
  115.5 0.0 reduce-scatter.6.cloned.1.call-update
  115.5 0.0 reduce-scatter.4.cloned.1.call-start
  115.6 0.0 all-gather.4.cloned.1.call-done
  115.6 10.4 %fusion.8 = f32[1536,896]{1,0:T(8,128)} fusion(bf16[1536,1792]{1,0:T(8,128)(2,1)} %all-gather.4.cloned.1.call-done, bf16[896,1792]{1,0:T(8,128)(2,1)} %param.8), kind=kOutput, calls=%fused_computation.12 | convolution fusion | flops 4932501504 | bytes 14221312 | tf_op jit(solution)/shard_map/dot_general | solution.py:27
  126.0 0.0 copy-start.2
  126.0 0.0 reduce-scatter.4.cloned.1.call-update
  126.0 0.0 all-gather.6.cloned.1.call-start
  126.0 81.3 %reduce-scatter.6.cloned.1.call-done = f32[192,896]{1,0:T(8,128)} async-done(((f32[1536,896]{1,0:T(8,128)}), f32[192,896]{1,0:T(8,128)}) %reduce-scatter.6.cloned.1.call-update) | async-done | bytes 688144 | tf_op jit(solution)/shard_map/reduce_scatter | solution.py:44
  207.3 95.8 %reduce-scatter.4.cloned.1.call-done = f32[192,896]{1,0:T(8,128)} async-done(((f32[1536,896]{1,0:T(8,128)}), f32[192,896]{1,0:T(8,128)}) %reduce-scatter.4.cloned.1.call-update) | async-done | bytes 688144 | tf_op jit(solution)/shard_map/reduce_scatter | solution.py:45
  303.1 0.0 copy-done.2
  303.1 2.7 convert_reduce_fusion
  305.8 0.0 all-gather.6.cloned.1.call-update
  305.8 0.0 all-gather.8.cloned.1.call-start
  305.8 0.7 all-gather.8.cloned.1.call-update
  306.5 0.0 reduce-scatter.8.cloned.1.call-start
  306.6 57.4 %all-gather.6.cloned.1.call-done = bf16[1536,896]{1,0:T(8,128)(2,1)} async-done(((bf16[192,896]{1,0:T(8,128)(2,1)}), bf16[1536,896]{1,0:T(8,128)(2,1)}) %all-gather.6.cloned.1.call-update) | async-done | bytes 2752528 | tf_op jit(solution)/shard_map/all_gather | solution.py:53
  363.9 9.9 %fusion.10 = f32[1536,1792]{1,0:T(8,128)} fusion(bf16[1536,896]{1,0:T(8,128)(2,1)} %all-gather.6.cloned.1.call-done, bf16[1792,896]{1,0:T(8,128)(2,1)S(1)} %copy-done), kind=kOutput, calls=%fused_computation.14 | convolution fusion | flops 4932501504 | bytes 16973824 | tf_op jit(solution)/shard_map/dot_general | solution.py:27
  373.8 0.0 reduce-scatter.8.cloned.1.call-update
  373.9 23.8 %psum.7 = f32[896]{0:T(1024)} all-reduce(f32[896]{0:T(1024)S(1)} %get-tuple-element.8), channel_id=1, replica_groups=mesh['row'=8,'col'=16] {'row'}, use_global_device_ids=true, to_apply=%region_4.0 | all-reduce | flops 896 | bytes 7168 | tf_op jit(solution)/shard_map/psum | solution.py:55
  397.6 11.6 %convolution_bitcast_fusion = f32[1792,896]{0,1:T(8,128)} fusion(bf16[1536,896]{1,0:T(8,128)(2,1)} %all-gather.6.cloned.1.call-done, bf16[1536,1792]{1,0:T(8,128)(2,1)} %bitcast.14), kind=kOutput, calls=%fused_computation | convolution fusion | flops 4932501504 | bytes 14680064 | tf_op jit(solution)/shard_map/dot_general | solution.py:21
  409.2 7.8 %copy.9 = f32[1792,896]{1,0:T(8,128)} copy(f32[1792,896]{0,1:T(8,128)} %convolution_bitcast_fusion) | data formatting | bytes 12845056
  417.0 13.2 %all-gather.8.cloned.1.call-done = bf16[1536,896]{1,0:T(8,128)(2,1)} async-done(((bf16[192,896]{1,0:T(8,128)(2,1)}), bf16[1536,896]{1,0:T(8,128)(2,1)}) %all-gather.8.cloned.1.call-update) | async-done | bytes 2752528 | tf_op jit(solution)/shard_map/all_gather | solution.py:52
  430.2 11.5 %fusion.11 = f32[896,1792]{1,0:T(8,128)} fusion(bf16[1536,896]{1,0:T(8,128)(2,1)} %all-gather.8.cloned.1.call-done, bf16[1536,1792]{1,0:T(8,128)(2,1)} %all-gather.4.cloned.1.call-done), kind=kOutput, calls=%fused_computation.15 | convolution fusion | flops 4932501504 | bytes 14680064 | tf_op jit(solution)/shard_map/dot_general | solution.py:21
  441.6 68.5 %reduce-scatter.8.cloned.1.call-done = f32[96,1792]{1,0:T(8,128)} async-done(((f32[1536,1792]{1,0:T(8,128)}), f32[96,1792]{1,0:T(8,128)}) %reduce-scatter.8.cloned.1.call-update) | async-done | bytes 688144 | tf_op jit(solution)/shard_map/reduce_scatter | solution.py:58
  510.1 1.9 convert_element_type.13
Async XLA Ops:
  8.0 99.9 %copy-start = (bf16[1792,896]{1,0:T(8,128)(2,1)S(1)}, bf16[1792,896]{1,0:T(8,128)(2,1)}, u32[]{:S(2)}) copy-start(bf16[1792,896]{1,0:T(8,128)(2,1)} %param.6) | copy-start | bytes 9633796
  8.0 107.6 %all-gather.4.cloned.1.call-start = ((), (), s32[]{:S(2)}) async-start(), calls=%async_computation.4 | async-start | bytes 5849088 | tf_op jit(solution)/shard_map/all_gather | solution.py:39
  8.7 198.6 %reduce-scatter.6.cloned.1.call-start = ((), (), s32[]{:S(2)}) async-start(), calls=%async_computation.6 | async-start | bytes 6193152 | tf_op jit(solution)/shard_map/reduce_scatter | solution.py:44
  105.5 2.4 copy-start.1
  115.5 187.6 %reduce-scatter.4.cloned.1.call-start = ((), (), s32[]{:S(2)}) async-start(), calls=%async_computation.5 | async-start | bytes 6193152 | tf_op jit(solution)/shard_map/reduce_scatter | solution.py:45
  126.0 177.1 %copy-start.2 = (f32[896]{0:T(1024)S(1)}, f32[896]{0:T(1024)}, u32[]{:S(2)}) copy-start(f32[896]{0:T(1024)} %param.7) | copy-start | bytes 10756
  126.0 237.9 %all-gather.6.cloned.1.call-start = ((), (), s32[]{:S(2)}) async-start(), calls=%async_computation.7 | async-start | bytes 3096576 | tf_op jit(solution)/shard_map/all_gather | solution.py:53
  305.8 124.4 %all-gather.8.cloned.1.call-start = ((), (), s32[]{:S(2)}) async-start(), calls=%async_computation.9 | async-start | bytes 3096576 | tf_op jit(solution)/shard_map/all_gather | solution.py:52
  306.5 203.6 %reduce-scatter.8.cloned.1.call-start = ((), (), s32[]{:S(2)}) async-start(), calls=%async_computation.8 | async-start | bytes 11698176 | tf_op jit(solution)/shard_map/reduce_scatter | solution.py:58
Sparse Core Ops, SparseCore 0:
  10.6 95.8 all-gather.3
  374.0 136.0 reduce-scatter.7
Sparse Core Ops, SparseCore 1:
  115.6 91.7 reduce-scatter.5
  212.1 90.9 reduce-scatter.3
  305.9 58.0 all-gather.5
  366.2 63.9 all-gather.7
